TPU v7x, 32 devices: a whole 2x2x4 slice. The times are simulated.
32 devices in a mesh: mode: 8 (over z, y), tm: 4 (over x, core).
Axes of the slice: x: 2, y: 2, z: 4, core: 2. Of those that a mesh axis runs over, the one named last changes fastest.
Arguments:
- support_accel: bfloat16 [512, 2048], P(None, 'tm'), may hold values from -6 to 6
- participation: bfloat16 [2048, 512], P('mode'), may hold values from -0.25 to 0.25
- kernels: float32 [2048, 2048], P('mode'), may hold values from -0.25 to 0.25
- lengths: int32 [2048], P('mode'), may hold values from 1 to 2048, as said below
- mode_shapes: bfloat16 [16384, 2048], P('mode'), may hold values from -0.125 to 0.125
- groups: int32 [16384], P('mode'), may hold values from 0 to 511
Outputs:
- response: bfloat16 [16384, 2048], P('mode', 'tm')
Inputs may be any that keep to these rules, and one draw needn't show every extreme that they name: `lengths`: some mode has exactly 2048 taps in every draw.
All inputs are finite; a program needn't handle non-finite values.
Results may differ from a plain program's by a relative error of at most 0.0033.
Values may be sent and summed in bfloat16 or wider, within the bound.
A program may use at most 64 MiB of HBM per device.

v0:
```python
import jax
import jax.numpy as jnp
from jax import lax
from jax.sharding import PartitionSpec as P


def passed_along(block, axis, distance):
    devices = range(lax.axis_size(axis))
    route = [(i - distance, i) for i in devices if i - distance in devices]
    return lax.ppermute(block, axis, route)


def depthwise(signal, weights):
    flipped = jnp.flip(weights, 1)[:, None, :]
    result = lax.conv_general_dilated(
        signal[None],
        flipped,
        (1,),
        "VALID",
        dimension_numbers=("NCH", "OIH", "NCH"),
        feature_group_count=signal.shape[0],
        precision=lax.Precision.HIGHEST,
    )
    return result[0]


def apply_filter(signal, kernel):
    return depthwise(signal, kernel)


def per_device(support_accel, participation, kernels, lengths, mode_shapes, groups):
    slab_len = support_accel.shape[1]
    tap_count = kernels.shape[1]
    depth_slabs = tap_count // slab_len
    forces = jnp.dot(participation, support_accel, preferred_element_type=jnp.float32)
    alive = jnp.arange(tap_count, dtype=jnp.int32)[None, :] < lengths[:, None]
    masked = jnp.where(alive, kernels, jnp.zeros_like(kernels))
    pieces = [forces]
    for distance in range(1, depth_slabs + 1):
        pieces.insert(0, passed_along(forces, "tm", distance))
    window = jnp.concatenate(pieces, axis=1)
    modal = apply_filter(window[:, 1:], masked).astype(jnp.bfloat16)
    initial = jnp.zeros((mode_shapes.shape[0], slab_len), jnp.float32)
    piece = jax.tree.map(lambda part: lax.all_gather(part, "mode", axis=0, tiled=True), modal)
    columns = lax.slice_in_dim(mode_shapes, 0, piece.shape[0], axis=1)
    summed = initial + jnp.dot(columns, piece, preferred_element_type=jnp.float32)
    ground = jnp.take(support_accel, groups, axis=0).astype(jnp.float32)
    return (summed + ground).astype(jnp.bfloat16)


def solution(mesh):
    placed = (
        P(None, "tm"),
        P("mode", None),
        P("mode", None),
        P("mode"),
        P("mode", None),
        P("mode"),
    )
    return jax.shard_map(
        per_device, mesh=mesh, in_specs=placed, out_specs=P("mode", "tm"), check_vma=False
    )
```

profile of v0, /device:TPU:0, one launch (start us, length us, event | category | flops | bytes accessed | tf_op | source)
XLA Modules:
  0.0 271.4 jit_solution(18268262673586640301)
XLA Ops:
  6.5 0.0 copy-start
  6.5 0.0 all-gather.3.cloned.1.call-start
  6.5 1.0 copy-done
  7.6 1.2 fusion.4
  8.8 1.5 collective-permute-start
  10.3 5.1 %collective-permute-start.1 = (f32[256,512]{1,0:T(8,128)S(1)}, f32[256,512]{1,0:T(8,128)}, u32[]{:S(2)}, u32[]{:S(2)}) collective-permute-start(f32[256,512]{1,0:T(8,128)S(1)} %fusion.4), channel_id=1, source_target_pairs={{0,3},{4,7},{8,11},{12,15},{16,19},{20,23},{24,27},{28,31}} | collective-permute-start | bytes 1572872 | tf_op jit(solution)/shard_map/ppermute | solution.py:10
  15.4 2.1 collective-permute-start.2
  17.5 2.1 collective-permute-start.3
  19.6 1.8 fusion.2
  21.4 11.6 %rev.4 = f32[256,2048]{1,0:T(8,128)} reverse(f32[256,2048]{1,0:T(8,128)S(1)} %fusion.2), dimensions={1} | reverse | bytes 4194304 | tf_op jit(solution)/shard_map/jit(_flip)/rev | solution.py:14
  33.0 6.1 %copy.12 = f32[256,1,2048]{0,1,2:T(1,128)} copy(f32[256,1,2048]{2,0,1:T(8,128)} %bitcast.15) | data formatting | bytes 4194304 | tf_op jit(solution)/shard_map/broadcast_in_dim | solution.py:14
  39.1 0.0 collective-permute-done
  39.1 1.1 constant_dynamic-update-slice_fusion.4
  40.2 0.0 collective-permute-done.1
  40.2 1.1 constant_dynamic-update-slice_fusion.3
  41.3 0.0 collective-permute-done.2
  41.3 1.1 constant_dynamic-update-slice_fusion.2
  42.3 0.0 collective-permute-done.3
  42.4 1.1 constant_dynamic-update-slice_fusion.1
  43.5 0.8 slice_bitcast_fusion
  44.2 4.0 %copy.11 = f32[1,256,2559]{1,0,2:T(1,128)} copy(f32[1,256,2559]{2,1,0:T(8,128)S(1)} %slice_bitcast_fusion) | data formatting | bytes 5240832 | tf_op jit(solution)/shard_map/broadcast_in_dim | solution.py:16
  48.3 0.0 copy-start.1
  48.3 90.9 %convolution_convert_fusion = bf16[1,256,512]{1,0,2:T(2,128)(2,1)} fusion(f32[1,256,2559]{1,0,2:T(1,128)} %copy.11, f32[256,1,2048]{0,1,2:T(1,128)} %copy.12), kind=kOutput, calls=%fused_computation.7 | convolution fusion | flops 3221356544 | bytes 4979712 | tf_op jit(solution)/shard_map/conv_general_dilated | solution.py:15
  139.1 0.0 all-gather.3.cloned.1.call-update
  139.2 0.0 copy-done.1
  139.2 7.5 %gather_fusion = bf16[2048,512]{1,0:T(8,128)(2,1)S(1)} fusion(bf16[512,512]{1,0:T(8,128)(2,1)S(1)} %copy-done, s32[2048]{0:T(1024)S(1)} %fusion.3), kind=kCustom, calls=%fused_computation | custom fusion | bytes 4202496 | tf_op jit(solution)/shard_map/jit(_take)/gather | solution.py:47
  146.7 2.4 copy.14
  149.1 92.8 %all-gather.3.cloned.1.call-done = bf16[1,2048,512]{1,0,2:T(2,128)(2,1)} async-done(((bf16[1,256,512]{1,0,2:T(2,128)(2,1)}), bf16[1,2048,512]{1,0,2:T(2,128)(2,1)}) %all-gather.3.cloned.1.call-update) | async-done | bytes 2097168 | tf_op jit(solution)/shard_map/all_gather | solution.py:44
  241.9 9.0 %copy.13 = bf16[1,2048,512]{2,1,0:T(8,128)(2,1)S(1)} copy(bf16[1,2048,512]{1,0,2:T(2,128)(2,1)} %all-gather.3.cloned.1.call-done) | data formatting | bytes 4194304 | tf_op jit(solution)/shard_map/all_gather | solution.py:44
  250.9 9.7 %fusion = bf16[2048,512]{0,1:T(8,128)(2,1)} fusion(bf16[2048,2048]{1,0:T(8,128)(2,1)} %param.10, bf16[1,2048,512]{2,1,0:T(8,128)(2,1)S(1)} %copy.13, bf16[2048,512]{0,1:T(8,128)(2,1)} %copy.14, pred[2048]{0:T(1024)(128)(4,1)S(1)} %compare_and_fusion), kind=kOutput, calls=%fused_computation.2 | convolution fusion | flops 4299161600 | bytes 14682112 | tf_op jit(solution)/shard_map/dot_general | solution.py:46
  260.6 3.9 %copy.15 = bf16[2048,512]{1,0:T(8,128)(2,1)} copy(bf16[2048,512]{0,1:T(8,128)(2,1)} %fusion) | data formatting | bytes 4194304 | tf_op jit(solution)/shard_map/convert_element_type | solution.py:48
  (3 shorter events, 0.1 us)
Async XLA Ops:
  6.5 1.0 copy-start
  6.5 235.4 %all-gather.3.cloned.1.call-start = ((), (), s32[]{:S(2)}) async-start(), calls=%async_computation | async-start | bytes 4718592 | tf_op jit(solution)/shard_map/all_gather | solution.py:44
  8.8 30.3 %collective-permute-start = (f32[256,512]{1,0:T(8,128)S(1)}, f32[256,512]{1,0:T(8,128)}, u32[]{:S(2)}, u32[]{:S(2)}) collective-permute-start(f32[256,512]{1,0:T(8,128)S(1)} %fusion.4), channel_id=1, source_target_pairs={} | collective-permute-start | bytes 1572872 | tf_op jit(solution)/shard_map/ppermute | solution.py:10
  10.3 29.9 %collective-permute-start.1 = (f32[256,512]{1,0:T(8,128)S(1)}, f32[256,512]{1,0:T(8,128)}, u32[]{:S(2)}, u32[]{:S(2)}) collective-permute-start(f32[256,512]{1,0:T(8,128)S(1)} %fusion.4), channel_id=1, source_target_pairs={{0,3},{4,7},{8,11},{12,15},{16,19},{20,23},{24,27},{28,31}} | collective-permute-start | bytes 1572872 | tf_op jit(solution)/shard_map/ppermute | solution.py:10
  15.4 25.9 %collective-permute-start.2 = (f32[256,512]{1,0:T(8,128)S(1)}, f32[256,512]{1,0:T(8,128)}, u32[]{:S(2)}, u32[]{:S(2)}) collective-permute-start(f32[256,512]{1,0:T(8,128)S(1)} %fusion.4), channel_id=1, source_target_pairs={{0,2},{1,3},{4,6},{5,7},{8,10},{9,11},{12,14},{13,15},{16,18},{17,... | collective-permute-start | bytes 1572872 | tf_op jit(solution)/shard_map/ppermute | solution.py:10
  17.5 24.9 %collective-permute-start.3 = (f32[256,512]{1,0:T(8,128)S(1)}, f32[256,512]{1,0:T(8,128)}, u32[]{:S(2)}, u32[]{:S(2)}) collective-permute-start(f32[256,512]{1,0:T(8,128)S(1)} %fusion.4), channel_id=1, source_target_pairs={{0,1},{1,2},{2,3},{4,5},{5,6},{6,7},{8,9},{9,10},{10,11},{12,13},{... | collective-permute-start | bytes 1572872 | tf_op jit(solution)/shard_map/ppermute | solution.py:10
  48.3 90.9 %copy-start.1 = (s32[2048]{0:T(1024)S(1)}, s32[2048]{0:T(1024)}, u32[]{:S(2)}) copy-start(s32[2048]{0:T(1024)} %param.11) | copy-start | bytes 24580
Sparse Core Ops, SparseCore 0:
  139.3 102.5 all-gather.2
where the time goes:
time: 272 us; the launch traced here: 271 us
  matrix products  102 us (38%)
  waiting for transfers between devices  92.8 us (34%)
  local copies, waits for them, and re-layouts  50.7 us (19%)
  between operations  13.5 us (5%)
  starting transfers between devices  10.8 us (4%)
    all_gather x1, waiting for transfers between devices, per_device(): lax.all_gather(part, 'mode', axis=0, tiled=True)  92.8 us
    conv_general_dilated x1, matrix products, depthwise(): lax.conv_general_dilated(signal[None], flipped, (1,), 'VALID', dimension_...  90.9 us
    rev x1, local copies, waits for them, and re-layouts, depthwise(): flipped = jnp.flip(weights, 1)[:, None, :]  11.6 us
    ppermute x4, starting transfers between devices, passed_along(): return lax.ppermute(block, axis, route)  10.7 us
    gather x2, local copies, waits for them, and re-layouts, per_device(): ground = jnp.take(support_accel, groups, axis=0).astype(jnp.float32)  9.92 us
    dot_general x1, matrix products, per_device(): jnp.dot(columns, piece, preferred_element_type=jnp.float32)  9.71 us
    all_gather x1, local copies, waits for them, and re-layouts, per_device(): lax.all_gather(part, 'mode', axis=0, tiled=True)  8.97 us
    broadcast_in_dim x1, local copies, waits for them, and re-layouts, depthwise(): flipped = jnp.flip(weights, 1)[:, None, :]  6.06 us
  transfers between devices with their start and end apart: 5, of which 1 were waited for; matrix products, arithmetic and copies ran while one was open for 12% of the time, Pallas kernels for 0%

commit v1 on v0

v1 whole, which is shorter than its diff:
```python
import functools

import jax
import jax.numpy as jnp
import numpy as np
from jax import lax
from jax.experimental import pallas as pl
from jax.experimental.pallas import tpu as pltpu
from jax.sharding import PartitionSpec as P

BLOCK = 128
F32 = jnp.float32
BF16 = jnp.bfloat16


def split_constant(table):
    high = table.astype(BF16)
    low = (table - high.astype(np.float64)).astype(BF16)
    return high, low


def transform_tables():
    angle = np.pi * (np.arange(BLOCK)[:, None] + 0.5) / BLOCK
    time = np.arange(2 * BLOCK)[None, :]
    cos, sin = np.cos(angle * time), np.sin(angle * time)
    forward = np.concatenate([cos[:, :BLOCK], -sin[:, :BLOCK]], axis=0).T
    backward = np.concatenate([cos, -sin], axis=0) / BLOCK
    return split_constant(forward) + split_constant(backward)


def dot3(values, high, low):
    top = values.astype(BF16)
    rest = (values - top.astype(F32)).astype(BF16)
    dot = functools.partial(jnp.dot, preferred_element_type=F32)
    return dot(top, high) + (dot(rest, high) + dot(top, low))


def filter_kernel(f_ref, k_ref, len_ref, fh_ref, fl_ref, bh_ref, bl_ref, y_ref, xs, fs, hs):
    rows, times = f_ref.shape
    taps = k_ref.shape[1]
    tblocks, kblocks = times // BLOCK, taps // BLOCK
    lengths = len_ref[...]
    for c in range(kblocks):
        pos = c * BLOCK + lax.broadcasted_iota(jnp.int32, (rows, BLOCK), 1)
        part = k_ref[:, c * BLOCK:(c + 1) * BLOCK]
        xs[c * rows:(c + 1) * rows, :] = jnp.where(pos < lengths, part, jnp.zeros_like(part))
    hs[...] = dot3(xs[:kblocks * rows, :], fh_ref[...], fl_ref[...])
    for a in range(tblocks):
        xs[a * rows:(a + 1) * rows, :] = f_ref[:, a * BLOCK:(a + 1) * BLOCK]
    fs[...] = dot3(xs[:tblocks * rows, :], fh_ref[...], fl_ref[...])
    before = jnp.zeros((rows, BLOCK), F32)
    for b in range(tblocks):
        re = jnp.zeros((rows, BLOCK), F32)
        im = jnp.zeros((rows, BLOCK), F32)
        for c in range(min(b + 1, kblocks)):
            fr = fs[(b - c) * rows:(b - c + 1) * rows, :BLOCK]
            fi = fs[(b - c) * rows:(b - c + 1) * rows, BLOCK:]
            hr = hs[c * rows:(c + 1) * rows, :BLOCK]
            hi = hs[c * rows:(c + 1) * rows, BLOCK:]
            re = re + (fr * hr - fi * hi)
            im = im + (fr * hi + fi * hr)
        wide = dot3(jnp.concatenate([re, im], axis=1), bh_ref[...], bl_ref[...])
        y_ref[:, b * BLOCK:(b + 1) * BLOCK] = (before + wide[:, :BLOCK]).astype(BF16)
        before = wide[:, BLOCK:]


def filtered(forces, kernels, lengths):
    rows, times = forces.shape
    taps = kernels.shape[1]
    tables = transform_tables()
    vmem = pl.BlockSpec(memory_space=pltpu.VMEM)
    return pl.pallas_call(
        filter_kernel,
        out_shape=jax.ShapeDtypeStruct((rows, times), BF16),
        in_specs=[vmem] * 7,
        out_specs=vmem,
        scratch_shapes=[
            pltpu.VMEM((max(times, taps) // BLOCK * rows, BLOCK), F32),
            pltpu.VMEM((times // BLOCK * rows, 2 * BLOCK), F32),
            pltpu.VMEM((taps // BLOCK * rows, 2 * BLOCK), F32),
        ],
        compiler_params=pltpu.CompilerParams(vmem_limit_bytes=32 << 20),
    )(forces, kernels, lengths[:, None], *map(jnp.asarray, tables))


def recover_kernel(g_ref, s_ref, m_ref, a_ref, o_ref):
    hot = lax.broadcasted_iota(jnp.int32, (g_ref.shape[0], a_ref.shape[0]), 1) == g_ref[...]
    ground = jnp.dot(hot.astype(F32).astype(BF16), a_ref[...], preferred_element_type=F32)
    summed = jnp.dot(s_ref[...], m_ref[...], preferred_element_type=F32)
    o_ref[...] = (summed + ground).astype(BF16)


def recovered(groups, mode_shapes, modal, support_accel):
    dofs, modes = mode_shapes.shape
    supports, slab = support_accel.shape
    tile = min(256, dofs)
    return pl.pallas_call(
        recover_kernel,
        grid=(dofs // tile,),
        out_shape=jax.ShapeDtypeStruct((dofs, slab), BF16),
        in_specs=[
            pl.BlockSpec((tile, 1), lambda i: (i, 0)),
            pl.BlockSpec((tile, modes), lambda i: (i, 0)),
            pl.BlockSpec((modes, slab), lambda i: (0, 0)),
            pl.BlockSpec((supports, slab), lambda i: (0, 0)),
        ],
        out_specs=pl.BlockSpec((tile, slab), lambda i: (i, 0)),
        compiler_params=pltpu.CompilerParams(vmem_limit_bytes=60 << 20),
    )(groups[:, None], mode_shapes, modal, support_accel)


def per_device(support_accel, participation, kernels, lengths, mode_shapes, groups):
    ways = lax.axis_size("tm")
    share = kernels.shape[0] // ways
    first = lax.axis_index("tm") * share
    forces = jnp.dot(participation, support_accel, preferred_element_type=F32)
    mine = lax.all_to_all(forces, "tm", split_axis=0, concat_axis=1, tiled=True)
    modal = filtered(
        mine,
        lax.dynamic_slice_in_dim(kernels, first, share, 0),
        lax.dynamic_slice_in_dim(lengths, first, share, 0),
    )
    slab = lax.all_to_all(modal, "tm", split_axis=1, concat_axis=0, tiled=True)
    every = lax.all_gather(slab, "mode", axis=0, tiled=True)
    return recovered(groups, mode_shapes, every, support_accel)


def solution(mesh):
    placed = (
        P(None, "tm"),
        P("mode", None),
        P("mode", None),
        P("mode"),
        P("mode", None),
        P("mode"),
    )
    return jax.shard_map(
        per_device, mesh=mesh, in_specs=placed, out_specs=P("mode", "tm"), check_vma=False
    )
```

time: 272 us -> 105 us (0.39)
  matrix products: 102 us -> 2.37 us
  local copies, waits for them, and re-layouts: 50.7 us -> 2.7 us
  waiting for transfers between devices: 92.8 us -> 58.2 us
  Pallas kernels: 0 us -> 14.2 us
  blocking collectives: 0 us -> 9.06 us
  starting transfers between devices: 10.8 us -> 4.24 us
    conv_general_dilated x1 -> x0, matrix products: 90.9 us -> none  [depthwise(): lax.conv_general_dilated(signal[None], flipped, (1,), 'VALID', dimension_...]
    all_gather x1, waiting for transfers between devices: 92.8 us -> 49 us  [per_device(): every = lax.all_gather(slab, 'mode', axis=0, tiled=True)]
    pallas_call x0 -> x2, Pallas kernels: none -> 14.2 us  [the longest x1 11.6 us: recovered(): pl.pallas_call(recover_kernel, grid=(dofs // tile,), out_shape=jax.ShapeD...]
    rev x1 -> x0, local copies, waits for them, and re-layouts: 11.6 us -> none  [depthwise(): flipped = jnp.flip(weights, 1)[:, None, :]]
    ppermute x4 -> x0, starting transfers between devices: 10.7 us -> none  [passed_along(): return lax.ppermute(block, axis, route)]
    gather x2 -> x0, local copies, waits for them, and re-layouts: 9.92 us -> none  [per_device(): ground = jnp.take(support_accel, groups, axis=0).astype(jnp.float32)]
    broadcast_in_dim x3, local copies, waits for them, and re-layouts: 10.8 us -> 1.54 us  [the longest x1 1.37 us: recovered(): groups[:, None]]
    all_to_all x0 -> x1, waiting for transfers between devices: none -> 9.2 us  [per_device(): mine = lax.all_to_all(forces, 'tm', split_axis=0, concat_axis=1, tiled=True)]
  transfers between devices with their start and end apart: 5 -> 2, of which waited for: 1 -> 2; matrix products, arithmetic and copies ran while one was open for 12% -> 2% of each run, Pallas kernels for 0% -> 0%
where the time goes in v1:
time: 105 us; the launch traced here: 104 us
  waiting for transfers between devices  58.2 us (55%)
  Pallas kernels  14.2 us (14%)
  between operations  13.5 us (13%)
  blocking collectives  9.06 us (9%)
  starting transfers between devices  4.24 us (4%)
  local copies, waits for them, and re-layouts  2.7 us (3%)
  matrix products  2.37 us (2%)
    all_gather x1, waiting for transfers between devices, per_device(): every = lax.all_gather(slab, 'mode', axis=0, tiled=True)  49 us
    pallas_call x1, Pallas kernels, recovered(): pl.pallas_call(recover_kernel, grid=(dofs // tile,), out_shape=jax.ShapeD...  11.6 us
    all_to_all x1, waiting for transfers between devices, per_device(): mine = lax.all_to_all(forces, 'tm', split_axis=0, concat_axis=1, tiled=True)  9.2 us
    all_to_all x1, blocking collectives, per_device(): slab = lax.all_to_all(modal, 'tm', split_axis=1, concat_axis=0, tiled=True)  9.06 us
    all_to_all x1, starting transfers between devices, per_device(): mine = lax.all_to_all(forces, 'tm', split_axis=0, concat_axis=1, tiled=True)  4.23 us
    pallas_call x1, Pallas kernels, filtered(): pl.pallas_call(filter_kernel, out_shape=jax.ShapeDtypeStruct((rows, times...  2.67 us
    dot_general x1, matrix products, per_device(): forces = jnp.dot(participation, support_accel, preferred_element_type=F32)  2.37 us
  transfers between devices with their start and end apart: 2, of which 2 were waited for; matrix products, arithmetic and copies ran while one was open for 2% of the time, Pallas kernels for 0%

profile of v1, /device:TPU:0, one launch (start us, length us, event | category | flops | bytes accessed | tf_op | source)
XLA Modules:
  0.0 104.3 jit_solution(12309006388940840262)
XLA Ops:
  6.5 0.0 copy-start
  6.5 0.0 copy-start.1
  6.5 0.0 copy-start.2
  6.5 0.0 copy-start.3
  6.5 0.0 copy-start.4
  6.6 0.0 copy-start.6
  6.6 2.4 %fusion = f32[256,512]{1,0:T(8,128)} fusion(bf16[256,512]{1,0:T(8,128)(2,1)} %param.11, bf16[512,512]{1,0:T(8,128)(2,1)} %a_ref.1), kind=kOutput, calls=%fused_computation.3 | convolution fusion | flops 134217728 | bytes 1310720 | tf_op jit(solution)/shard_map/dot_general | solution.py:116
  8.9 4.2 %all-to-all-start = ((f32[4,64,512]{2,1,0:T(8,128)}), f32[4,64,512]{2,1,0:T(8,128)}, u32[]{:S(2)}, u32[]{:S(2)}) async-start(f32[4,64,512]{2,1,0:T(8,128)} %bitcast.1), calls=%async_computation | async-start | bytes 1048576 | tf_op jit(solution)/shard_map/all_to_all | solution.py:117
  13.2 0.0 all-gather.2.cloned.1.call-start
  13.2 0.0 copy-done.6
  13.2 0.1 dynamic-slice_bitcast_fusion
  13.2 0.1 copy.19.len_ref
  13.3 0.0 copy-done
  13.4 0.0 copy-start.5
  13.4 9.2 %all-to-all-done = f32[4,64,512]{2,1,0:T(8,128)} async-done(((f32[4,64,512]{2,1,0:T(8,128)}), f32[4,64,512]{2,1,0:T(8,128)}, u32[]{:S(2)}, u32[]{:S(2)}) %all-to-all-start) | async-done | bytes 524320 | tf_op jit(solution)/shard_map/all_to_all | solution.py:117
  22.6 1.1 %copy.23 = f32[4,8,8,512]{3,2,0,1:T(8,128)S(1)} copy(f32[4,8,8,512]{3,2,1,0:T(8,128)} %bitcast.9) | data formatting | bytes 1048576 | tf_op jit(solution)/shard_map/all_to_all | solution.py:117
  23.7 0.0 copy-done.1
  23.7 0.0 copy-done.2
  23.7 0.0 copy-done.3
  23.7 0.0 copy-done.4
  23.7 2.7 %shard_map.100 = bf16[64,2048]{1,0:T(8,128)(2,1)S(1)} custom-call(f32[64,2048]{1,0:T(8,128)S(1)} %bitcast.16, f32[64,2048]{1,0:T(8,128)S(1)} %constant_dynamic-slice_fusion.k_ref, s32[64,1]{1,0:T(8,128)S(1)} %copy.19.len_ref, bf16[128,256]{1,0:T(8,128)(2,1)S(1)} %copy-done.4, bf16[128,256]{1,0:T(8,128)(2,1)S(1)} %copy-done.3, ...), custom_call_target="tpu_custom_call" | custom-call | tf_op jit(solution)/shard_map/pallas_call | solution.py:72
  26.4 9.1 %all_to_all.38 = bf16[64,4,512]{2,0,1:T(8,128)(2,1)} all-to-all(bf16[64,4,512]{2,0,1:T(8,128)(2,1)S(1)} %bitcast.19), channel_id=1, replica_groups=mesh['mode'=8,'tm'=4] {'tm'}, dimensions={1} | all-to-all | bytes 524288 | tf_op jit(solution)/shard_map/all_to_all | solution.py:123
  35.5 0.0 all-gather.2.cloned.1.call-update
  35.5 0.0 copy-done.5
  35.5 1.4 %copy.21.g_ref = s32[2048,1]{1,0:T(8,128)} copy(s32[2048,1]{0,1:T(1,128)S(1)} %bitcast.20) | data formatting | bytes 16384 | tf_op jit(solution)/shard_map/broadcast_in_dim | solution.py:109
  36.9 49.0 %all-gather.2.cloned.1.call-done.m_ref = bf16[2048,512]{1,0:T(8,128)(2,1)} async-done(((bf16[256,512]{1,0:T(8,128)(2,1)}), bf16[2048,512]{1,0:T(8,128)(2,1)}) %all-gather.2.cloned.1.call-update) | async-done | bytes 2097168 | tf_op jit(solution)/shard_map/all_gather | solution.py:124
  85.9 11.6 %shard_map.101 = bf16[2048,512]{1,0:T(8,128)(2,1)} custom-call(s32[2048,1]{1,0:T(8,128)} %copy.21.g_ref, bf16[2048,2048]{1,0:T(8,128)(2,1)} %s_ref.1, bf16[2048,512]{1,0:T(8,128)(2,1)} %all-gather.2.cloned.1.call-done.m_ref, bf16[512,512]{1,0:T(8,128)(2,1)} %a_ref.1), custom_call_target="tpu_custom_call" | custom-call | tf_op jit(solution)/shard_map/pallas_call | solution.py:97
  (2 shorter events, 0.1 us)
Async XLA Ops:
  6.5 6.8 %copy-start = (f32[256,2048]{1,0:T(8,128)S(1)}, f32[256,2048]{1,0:T(8,128)}, u32[]{:S(2)}) copy-start(f32[256,2048]{1,0:T(8,128)} %param.12) | copy-start | bytes 6291460
  6.5 17.2 %copy-start.1 = (bf16[256,256]{1,0:T(8,128)(2,1)S(1)}, bf16[256,256]{1,0:T(8,128)(2,1)}, u32[]{:S(2)}) copy-start(bf16[256,256]{1,0:T(8,128)(2,1)} %constant.21.clone.bl_ref) | copy-start | bytes 393220
  6.5 17.2 %copy-start.2 = (bf16[256,256]{1,0:T(8,128)(2,1)S(1)}, bf16[256,256]{1,0:T(8,128)(2,1)}, u32[]{:S(2)}) copy-start(bf16[256,256]{1,0:T(8,128)(2,1)} %constant.20.clone.bh_ref) | copy-start | bytes 393220
  6.5 17.2 %copy-start.3 = (bf16[128,256]{1,0:T(8,128)(2,1)S(1)}, bf16[128,256]{1,0:T(8,128)(2,1)}, u32[]{:S(2)}) copy-start(bf16[128,256]{1,0:T(8,128)(2,1)} %constant.19.clone.fl_ref) | copy-start | bytes 196612
  6.5 17.2 %copy-start.4 = (bf16[128,256]{1,0:T(8,128)(2,1)S(1)}, bf16[128,256]{1,0:T(8,128)(2,1)}, u32[]{:S(2)}) copy-start(bf16[128,256]{1,0:T(8,128)(2,1)} %constant.18.clone.fh_ref) | copy-start | bytes 196612
  6.6 6.6 %copy-start.6 = (s32[256]{0:T(256)S(1)}, s32[256]{0:T(256)}, u32[]{:S(2)}) copy-start(s32[256]{0:T(256)} %param.13) | copy-start | bytes 3076
  8.9 13.7 %all-to-all-start = ((f32[4,64,512]{2,1,0:T(8,128)}), f32[4,64,512]{2,1,0:T(8,128)}, u32[]{:S(2)}, u32[]{:S(2)}) async-start(f32[4,64,512]{2,1,0:T(8,128)} %bitcast.1), calls=%async_computation | async-start | bytes 1048576 | tf_op jit(solution)/shard_map/all_to_all | solution.py:117
  13.2 72.7 %all-gather.2.cloned.1.call-start = ((), (), s32[]{:S(2)}) async-start(), calls=%async_computation.2 | async-start | bytes 2359296 | tf_op jit(solution)/shard_map/all_gather | solution.py:124
  13.4 22.1 %copy-start.5 = (s32[2048]{0:T(1024)S(1)}, s32[2048]{0:T(1024)}, u32[]{:S(2)}) copy-start(s32[2048]{0:T(1024)} %param.15) | copy-start | bytes 24580
Sparse Core Ops, SparseCore 0:
  35.6 50.1 all-gather.1

commit v2 on v1

--- a/solution.py
+++ b/solution.py
@@ -83,6 +83,201 @@
     )(forces, kernels, lengths[:, None], *map(jnp.asarray, tables))
 
 
+MESH = pl.DeviceIdType.MESH
+
+
+def exchange_kernel(f_ref, o_ref, own_sem, send_sems, recv_sems):
+    ways, _, slab = f_ref.shape
+    i, j = lax.axis_index("mode"), lax.axis_index("tm")
+    barrier = pltpu.get_barrier_semaphore()
+    for d in range(1, ways):
+        peer = {"mode": i, "tm": lax.rem(j + d, ways)}
+        pl.semaphore_signal(barrier, inc=1, device_id=peer, device_id_type=MESH)
+    pl.semaphore_wait(barrier, ways - 1)
+    own = o_ref.at[:, pl.ds(pl.multiple_of(j * slab, slab), slab)]
+    copies = [pltpu.make_async_copy(f_ref.at[j], own, own_sem)]
+    for d in range(ways - 1, 0, -1):
+        t = lax.rem(j + d, ways)
+        copies.append(pltpu.make_async_remote_copy(
+            f_ref.at[t], own, send_sems.at[d - 1], recv_sems.at[d - 1],
+            device_id={"mode": i, "tm": t}, device_id_type=MESH,
+        ))
+    for copy in copies:
+        copy.start()
+    for copy in copies:
+        copy.wait()
+
+
+def exchanged(forces, ways):
+    rows, slab = forces.shape
+    share = rows // ways
+    vmem = pl.BlockSpec(memory_space=pltpu.VMEM)
+    return pl.pallas_call(
+        exchange_kernel,
+        out_shape=jax.ShapeDtypeStruct((share, ways * slab), forces.dtype),
+        in_specs=[vmem],
+        out_specs=vmem,
+        scratch_shapes=[
+            pltpu.SemaphoreType.DMA,
+            pltpu.SemaphoreType.DMA((ways - 1,)),
+            pltpu.SemaphoreType.DMA((ways - 1,)),
+        ],
+        compiler_params=pltpu.CompilerParams(
+            collective_id=0, has_side_effects=True, vmem_limit_bytes=32 << 20
+        ),
+    )(forces.reshape(ways, share, slab))
+
+
+def gather_kernel(ny, m_ref, o_ref, own_sem, s1, r1, s_up, r_up, s_down, r_down, s_y, r_y):
+    groups, ways, _, slab = o_ref.shape
+    nz = groups // ny
+    i, j = lax.axis_index("mode"), lax.axis_index("tm")
+    z, y = i // ny, lax.rem(i, ny)
+    below, above = z > 0, z < nz - 1
+
+    def greet(mode, tm):
+        peer = {"mode": mode, "tm": tm}
+        pl.semaphore_signal(barrier, inc=1, device_id=peer, device_id_type=MESH)
+
+    barrier = pltpu.get_barrier_semaphore()
+    for d in range(1, ways):
+        greet(i, lax.rem(j + d, ways))
+    for d in range(1, ny):
+        greet(z * ny + lax.rem(y + d, ny), j)
+
+    @pl.when(below)
+    def _():
+        greet(i - ny, j)
+
+    @pl.when(above)
+    def _():
+        greet(i + ny, j)
+
+    always = ways - 1 + ny - 1
+    if nz == 1:
+        pl.semaphore_wait(barrier, always)
+    else:
+        @pl.when(below & above)
+        def _():
+            pl.semaphore_wait(barrier, always + 2)
+
+        @pl.when(jnp.logical_not(below & above))
+        def _():
+            pl.semaphore_wait(barrier, always + 1)
+
+    mine = m_ref.at[:, pl.ds(pl.multiple_of(j * slab, slab), slab)]
+    first = [pltpu.make_async_copy(mine, o_ref.at[i, j], own_sem)]
+    for d in range(ways - 1, 0, -1):
+        t = lax.rem(j + d, ways)
+        first.append(pltpu.make_async_remote_copy(
+            m_ref.at[:, pl.ds(pl.multiple_of(t * slab, slab), slab)], o_ref.at[i, j],
+            s1.at[d - 1], r1.at[d - 1], device_id={"mode": i, "tm": t}, device_id_type=MESH,
+        ))
+    for copy in first:
+        copy.start()
+    for copy in first:
+        copy.wait()
+
+    def move(block, send, recv, mode):
+        return pltpu.make_async_remote_copy(
+            o_ref.at[block], o_ref.at[block], send, recv,
+            device_id={"mode": mode, "tm": j}, device_id_type=MESH,
+        )
+
+    def up(step, block):
+        return move(block, s_up.at[step], r_up.at[step], i + ny)
+
+    def down(step, block):
+        return move(block, s_down.at[step], r_down.at[step], i - ny)
+
+    def across(slot, line, column, d):
+        return move(line * ny + column, s_y.at[slot, d - 1], r_y.at[slot, d - 1], z * ny + lax.rem(y + d, ny))
+
+    def across_start(slot, line):
+        for d in range(1, ny):
+            across(slot, line, y, d).start()
+
+    def across_wait(slot, line):
+        for d in range(1, ny):
+            across(slot, line, y, d).wait_send()
+            across(slot, line, lax.rem(y + ny - d, ny), d).wait_recv()
+
+    @pl.when(above)
+    def _():
+        up(0, i).start()
+
+    @pl.when(below)
+    def _():
+        down(0, i).start()
+
+    across_start(0, z)
+    for step in range(nz - 1):
+        @pl.when(z - 1 - step >= 0)
+        def _(step=step):
+            block = i - (1 + step) * ny
+            move(block, s_up.at[step], r_up.at[step], i - ny).wait_recv()
+            if step + 1 < nz - 1:
+                @pl.when(above)
+                def _():
+                    up(step + 1, block).start()
+            across_start(1 + 2 * step, z - 1 - step)
+
+        @pl.when(z + 1 + step <= nz - 1)
+        def _(step=step):
+            block = i + (1 + step) * ny
+            move(block, s_down.at[step], r_down.at[step], i + ny).wait_recv()
+            if step + 1 < nz - 1:
+                @pl.when(below)
+                def _():
+                    down(step + 1, block).start()
+            across_start(2 + 2 * step, z + 1 + step)
+
+    across_wait(0, z)
+    for step in range(nz - 1):
+        @pl.when((z - step >= 0) & above)
+        def _(step=step):
+            up(step, i - step * ny).wait_send()
+
+        @pl.when((z + step <= nz - 1) & below)
+        def _(step=step):
+            down(step, i + step * ny).wait_send()
+
+        @pl.when(z - 1 - step >= 0)
+        def _(step=step):
+            across_wait(1 + 2 * step, z - 1 - step)
+
+        @pl.when(z + 1 + step <= nz - 1)
+        def _(step=step):
+            across_wait(2 + 2 * step, z + 1 + step)
+
+
+def gathered(modal, groups, ways):
+    share, times = modal.shape
+    slab = times // ways
+    ny = max(ways // 2, 1)
+    if groups % ny:
+        ny = 1
+    nz = groups // ny
+    vmem = pl.BlockSpec(memory_space=pltpu.VMEM)
+    dma = pltpu.SemaphoreType.DMA
+    steps, others = max(nz - 1, 1), max(ny - 1, 1)
+    every = pl.pallas_call(
+        functools.partial(gather_kernel, ny),
+        out_shape=jax.ShapeDtypeStruct((groups, ways, share, slab), modal.dtype),
+        in_specs=[vmem],
+        out_specs=vmem,
+        scratch_shapes=[
+            dma, dma((ways - 1,)), dma((ways - 1,)),
+            dma((steps,)), dma((steps,)), dma((steps,)), dma((steps,)),
+            dma((1 + 2 * steps, others)), dma((1 + 2 * steps, others)),
+        ],
+        compiler_params=pltpu.CompilerParams(
+            collective_id=1, has_side_effects=True, vmem_limit_bytes=32 << 20
+        ),
+    )(modal)
+    return every.reshape(groups * ways * share, slab)
+
+
 def recover_kernel(g_ref, s_ref, m_ref, a_ref, o_ref):
     hot = lax.broadcasted_iota(jnp.int32, (g_ref.shape[0], a_ref.shape[0]), 1) == g_ref[...]
     ground = jnp.dot(hot.astype(F32).astype(BF16), a_ref[...], preferred_element_type=F32)
@@ -114,14 +309,13 @@
     share = kernels.shape[0] // ways
     first = lax.axis_index("tm") * share
     forces = jnp.dot(participation, support_accel, preferred_element_type=F32)
-    mine = lax.all_to_all(forces, "tm", split_axis=0, concat_axis=1, tiled=True)
+    mine = exchanged(forces, ways)
     modal = filtered(
         mine,
         lax.dynamic_slice_in_dim(kernels, first, share, 0),
         lax.dynamic_slice_in_dim(lengths, first, share, 0),
     )
-    slab = lax.all_to_all(modal, "tm", split_axis=1, concat_axis=0, tiled=True)
-    every = lax.all_gather(slab, "mode", axis=0, tiled=True)
+    every = gathered(modal, lax.axis_size("mode"), ways)
     return recovered(groups, mode_shapes, every, support_accel)
 
 

time: 105 us -> 62.9 us (0.60)
  waiting for transfers between devices: 58.2 us -> 0 us
  Pallas kernels: 14.2 us -> 56.7 us
  between operations: 13.5 us -> 0.11 us
  blocking collectives: 9.06 us -> 0 us
  starting transfers between devices: 4.24 us -> 0 us
  local copies, waits for them, and re-layouts: 2.7 us -> 4.36 us
    all_gather x1 -> x0, waiting for transfers between devices: 49 us -> none  [per_device(): every = lax.all_gather(slab, 'mode', axis=0, tiled=True)]
    pallas_call x0 -> x2, Pallas kernels: none -> 42.4 us  [the longest x1 32.4 us: gathered(): pl.pallas_call(functools.partial(gather_kernel, ny), out_shape=jax.ShapeD...]
    all_to_all x1 -> x0, waiting for transfers between devices: 9.2 us -> none  [per_device(): mine = lax.all_to_all(forces, 'tm', split_axis=0, concat_axis=1, tiled=True)]
    all_to_all x1 -> x0, blocking collectives: 9.06 us -> none  [per_device(): slab = lax.all_to_all(modal, 'tm', split_axis=1, concat_axis=0, tiled=True)]
    all_to_all x1 -> x0, starting transfers between devices: 4.23 us -> none  [per_device(): mine = lax.all_to_all(forces, 'tm', split_axis=0, concat_axis=1, tiled=True)]
    unnamed x14, local copies, waits for them, and re-layouts: 0.03 us -> 1.95 us
    all_to_all x2 -> x0, local copies, waits for them, and re-layouts: 1.09 us -> none  [the longest x1 1.08 us: per_device(): mine = lax.all_to_all(forces, 'tm', split_axis=0, concat_axis=1, tiled=True)]
  transfers between devices with their start and end apart: 2 -> 0, of which waited for: 2 -> 0; matrix products, arithmetic and copies ran while one was open for 2% -> 0% of each run, Pallas kernels for 0% -> 0%
where the time goes in v2:
time: 62.9 us; the launch traced here: 62.5 us
  Pallas kernels  56.7 us (90%)
  local copies, waits for them, and re-layouts  4.36 us (7%)
  matrix products  1.42 us (2%)
    pallas_call x1, Pallas kernels, gathered(): pl.pallas_call(functools.partial(gather_kernel, ny), out_shape=jax.ShapeD...  32.4 us
    pallas_call x1, Pallas kernels, recovered(): pl.pallas_call(recover_kernel, grid=(dofs // tile,), out_shape=jax.ShapeD...  11.6 us
    pallas_call x1, Pallas kernels, exchanged(): pl.pallas_call(exchange_kernel, out_shape=jax.ShapeDtypeStruct((share, wa...  10 us
    pallas_call x1, Pallas kernels, filtered(): pl.pallas_call(filter_kernel, out_shape=jax.ShapeDtypeStruct((rows, times...  2.67 us
    unnamed x14, local copies, waits for them, and re-layouts  1.95 us
    dot_general x1, matrix products, per_device(): forces = jnp.dot(participation, support_accel, preferred_element_type=F32)  1.42 us
    broadcast_in_dim x1, local copies, waits for them, and re-layouts, recovered(): groups[:, None]  1.38 us

profile of v2, /device:TPU:0, one launch (start us, length us, event | category | flops | bytes accessed | tf_op | source)
XLA Modules:
  0.0 62.5 jit_solution(9607978161426879613)
XLA Ops:
  0.0 0.0 copy-start
  0.0 0.0 copy-start.2
  0.0 0.0 copy-start.3
  0.0 0.0 copy-start.4
  0.0 0.0 copy-start.5
  0.0 0.9 %dynamic-slice_bitcast_fusion = s32[64,1]{0,1:T(1,128)S(1)} fusion(s32[256]{0:T(256)} %param.13, s32[]{:T(128)S(6)} %select_n.4), kind=kLoop, calls=%fused_computation | loop fusion | bytes 516 | tf_op jit(solution)/shard_map/broadcast_in_dim | solution.py:83
  0.9 0.1 copy.12.len_ref
  1.0 0.6 copy-done
  1.6 0.0 copy-start.6
  1.7 1.4 %fusion = f32[256,512]{1,0:T(8,128)S(1)} fusion(bf16[256,512]{1,0:T(8,128)(2,1)} %param.11, bf16[512,512]{1,0:T(8,128)(2,1)} %a_ref.1), kind=kOutput, calls=%fused_computation.2 | convolution fusion | flops 134217728 | bytes 1310720 | tf_op jit(solution)/shard_map/dot_general | solution.py:311
  3.1 10.0 %shard_map.100.f_ref = f32[64,2048]{1,0:T(8,128)S(1)} custom-call(f32[4,64,512]{2,1,0:T(8,128)S(1)} %bitcast.8), custom_call_target="tpu_custom_call" | custom-call | tf_op jit(solution)/shard_map/pallas_call | solution.py:115
  13.1 0.0 copy-done.2
  13.2 0.0 copy-done.3
  13.2 0.0 copy-done.4
  13.2 0.0 copy-done.5
  13.2 2.7 %shard_map.101.m_ref = bf16[64,2048]{1,0:T(8,128)(2,1)S(1)} custom-call(f32[64,2048]{1,0:T(8,128)S(1)} %shard_map.100.f_ref, f32[64,2048]{1,0:T(8,128)S(1)} %constant_dynamic-slice_fusion.k_ref, s32[64,1]{1,0:T(8,128)S(1)} %copy.12.len_ref, bf16[128,256]{1,0:T(8,128)(2,1)S(1)} %copy-done.5, bf16[128,256]{1,0:T(8,128)(2,1)S(1)} %copy-done.4, ...), custom_call_target="tpu_custom_call" | custom-call | tf_op jit(solution)/shard_map/pallas_call | solution.py:72
  15.9 0.0 copy-done.6
  15.9 1.4 %copy.13.g_ref = s32[2048,1]{1,0:T(8,128)} copy(s32[2048,1]{0,1:T(1,128)S(1)} %bitcast.9) | data formatting | bytes 16384 | tf_op jit(solution)/shard_map/broadcast_in_dim | solution.py:304
  17.3 32.4 %shard_map.102 = bf16[8,4,64,512]{3,2,1,0:T(8,128)(2,1)S(1)} custom-call(bf16[64,2048]{1,0:T(8,128)(2,1)S(1)} %shard_map.101.m_ref), custom_call_target="tpu_custom_call" | custom-call | tf_op jit(solution)/shard_map/pallas_call | solution.py:264
  49.6 0.0 copy-start.1
  49.6 1.3 %copy-done.1 = bf16[8,4,64,512]{3,2,1,0:T(8,128)(2,1)} copy-done((bf16[8,4,64,512]{3,2,1,0:T(8,128)(2,1)}, bf16[8,4,64,512]{3,2,1,0:T(8,128)(2,1)S(1)}, u32[]{:S(2)}) %copy-start.1) | copy-done | bytes 2097176
  51.0 11.6 %shard_map.103 = bf16[2048,512]{1,0:T(8,128)(2,1)} custom-call(s32[2048,1]{1,0:T(8,128)} %copy.13.g_ref, bf16[2048,2048]{1,0:T(8,128)(2,1)} %s_ref.1, bf16[2048,512]{1,0:T(8,128)(2,1)} %bitcast.7, bf16[512,512]{1,0:T(8,128)(2,1)} %a_ref.1), custom_call_target="tpu_custom_call" | custom-call | tf_op jit(solution)/shard_map/pallas_call | solution.py:292
  (1 shorter events, 0.0 us)
Async XLA Ops:
  0.0 1.6 %copy-start = (f32[256,2048]{1,0:T(8,128)S(1)}, f32[256,2048]{1,0:T(8,128)}, u32[]{:S(2)}) copy-start(f32[256,2048]{1,0:T(8,128)} %param.12) | copy-start | bytes 6291460
  0.0 13.1 %copy-start.2 = (bf16[256,256]{1,0:T(8,128)(2,1)S(1)}, bf16[256,256]{1,0:T(8,128)(2,1)}, u32[]{:S(2)}) copy-start(bf16[256,256]{1,0:T(8,128)(2,1)} %constant.21.clone.bl_ref) | copy-start | bytes 393220
  0.0 13.1 %copy-start.3 = (bf16[256,256]{1,0:T(8,128)(2,1)S(1)}, bf16[256,256]{1,0:T(8,128)(2,1)}, u32[]{:S(2)}) copy-start(bf16[256,256]{1,0:T(8,128)(2,1)} %constant.20.clone.bh_ref) | copy-start | bytes 393220
  0.0 13.2 %copy-start.4 = (bf16[128,256]{1,0:T(8,128)(2,1)S(1)}, bf16[128,256]{1,0:T(8,128)(2,1)}, u32[]{:S(2)}) copy-start(bf16[128,256]{1,0:T(8,128)(2,1)} %constant.19.clone.fl_ref) | copy-start | bytes 196612
  0.0 13.2 %copy-start.5 = (bf16[128,256]{1,0:T(8,128)(2,1)S(1)}, bf16[128,256]{1,0:T(8,128)(2,1)}, u32[]{:S(2)}) copy-start(bf16[128,256]{1,0:T(8,128)(2,1)} %constant.18.clone.fh_ref) | copy-start | bytes 196612
  1.6 14.2 %copy-start.6 = (s32[2048]{0:T(1024)S(1)}, s32[2048]{0:T(1024)}, u32[]{:S(2)}) copy-start(s32[2048]{0:T(1024)} %param.15) | copy-start | bytes 24580
  49.6 1.4 %copy-start.1 = (bf16[8,4,64,512]{3,2,1,0:T(8,128)(2,1)}, bf16[8,4,64,512]{3,2,1,0:T(8,128)(2,1)S(1)}, u32[]{:S(2)}) copy-start(bf16[8,4,64,512]{3,2,1,0:T(8,128)(2,1)S(1)} %shard_map.102) | copy-start | bytes 6291460

commit v3 on v2

--- a/solution.py
+++ b/solution.py
@@ -288,7 +288,7 @@
 def recovered(groups, mode_shapes, modal, support_accel):
     dofs, modes = mode_shapes.shape
     supports, slab = support_accel.shape
-    tile = min(256, dofs)
+    tile = min(512, dofs)
     return pl.pallas_call(
         recover_kernel,
         grid=(dofs // tile,),
@@ -300,7 +300,7 @@
             pl.BlockSpec((supports, slab), lambda i: (0, 0)),
         ],
         out_specs=pl.BlockSpec((tile, slab), lambda i: (i, 0)),
-        compiler_params=pltpu.CompilerParams(vmem_limit_bytes=60 << 20),
+        compiler_params=pltpu.CompilerParams(vmem_limit_bytes=57 << 20),
     )(groups[:, None], mode_shapes, modal, support_accel)
 
 

time: 62.9 us -> 61.1 us (0.971)
  Pallas kernels: 56.7 us -> 54.9 us
    pallas_call x1, Pallas kernels: 11.6 us -> 9.84 us  [recovered(): pl.pallas_call(recover_kernel, grid=(dofs // tile,), out_shape=jax.ShapeD...]
where the time goes in v3:
time: 61.1 us; the launch traced here: 60.8 us
  Pallas kernels  54.9 us (90%)
  local copies, waits for them, and re-layouts  4.36 us (7%)
  matrix products  1.42 us (2%)
    pallas_call x1, Pallas kernels, gathered(): pl.pallas_call(functools.partial(gather_kernel, ny), out_shape=jax.ShapeD...  32.4 us
    pallas_call x1, Pallas kernels, exchanged(): pl.pallas_call(exchange_kernel, out_shape=jax.ShapeDtypeStruct((share, wa...  10 us
    pallas_call x1, Pallas kernels, recovered(): pl.pallas_call(recover_kernel, grid=(dofs // tile,), out_shape=jax.ShapeD...  9.84 us
    pallas_call x1, Pallas kernels, filtered(): pl.pallas_call(filter_kernel, out_shape=jax.ShapeDtypeStruct((rows, times...  2.67 us
    unnamed x14, local copies, waits for them, and re-layouts  1.95 us
    dot_general x1, matrix products, per_device(): forces = jnp.dot(participation, support_accel, preferred_element_type=F32)  1.42 us
    broadcast_in_dim x1, local copies, waits for them, and re-layouts, recovered(): groups[:, None]  1.38 us

profile of v3, /device:TPU:0, one launch (start us, length us, event | category | flops | bytes accessed | tf_op | source)
XLA Modules:
  0.0 60.8 jit_solution(209767806151687076)
XLA Ops:
  0.0 0.0 copy-start
  0.0 0.0 copy-start.2
  0.0 0.0 copy-start.3
  0.0 0.0 copy-start.4
  0.0 0.0 copy-start.5
  0.0 0.9 %dynamic-slice_bitcast_fusion = s32[64,1]{0,1:T(1,128)S(1)} fusion(s32[256]{0:T(256)} %param.13, s32[]{:T(128)S(6)} %select_n.4), kind=kLoop, calls=%fused_computation | loop fusion | bytes 516 | tf_op jit(solution)/shard_map/broadcast_in_dim | solution.py:83
  0.9 0.1 copy.12.len_ref
  1.0 0.6 copy-done
  1.6 0.0 copy-start.6
  1.7 1.4 %fusion = f32[256,512]{1,0:T(8,128)S(1)} fusion(bf16[256,512]{1,0:T(8,128)(2,1)} %param.11, bf16[512,512]{1,0:T(8,128)(2,1)} %a_ref.1), kind=kOutput, calls=%fused_computation.2 | convolution fusion | flops 134217728 | bytes 1310720 | tf_op jit(solution)/shard_map/dot_general | solution.py:311
  3.1 10.0 %shard_map.100.f_ref = f32[64,2048]{1,0:T(8,128)S(1)} custom-call(f32[4,64,512]{2,1,0:T(8,128)S(1)} %bitcast.8), custom_call_target="tpu_custom_call" | custom-call | tf_op jit(solution)/shard_map/pallas_call | solution.py:115
  13.1 0.0 copy-done.2
  13.2 0.0 copy-done.3
  13.2 0.0 copy-done.4
  13.2 0.0 copy-done.5
  13.2 2.7 %shard_map.101.m_ref = bf16[64,2048]{1,0:T(8,128)(2,1)S(1)} custom-call(f32[64,2048]{1,0:T(8,128)S(1)} %shard_map.100.f_ref, f32[64,2048]{1,0:T(8,128)S(1)} %constant_dynamic-slice_fusion.k_ref, s32[64,1]{1,0:T(8,128)S(1)} %copy.12.len_ref, bf16[128,256]{1,0:T(8,128)(2,1)S(1)} %copy-done.5, bf16[128,256]{1,0:T(8,128)(2,1)S(1)} %copy-done.4, ...), custom_call_target="tpu_custom_call" | custom-call | tf_op jit(solution)/shard_map/pallas_call | solution.py:72
  15.9 0.0 copy-done.6
  15.9 1.4 %copy.13.g_ref = s32[2048,1]{1,0:T(8,128)} copy(s32[2048,1]{0,1:T(1,128)S(1)} %bitcast.9) | data formatting | bytes 16384 | tf_op jit(solution)/shard_map/broadcast_in_dim | solution.py:304
  17.3 32.4 %shard_map.102 = bf16[8,4,64,512]{3,2,1,0:T(8,128)(2,1)S(1)} custom-call(bf16[64,2048]{1,0:T(8,128)(2,1)S(1)} %shard_map.101.m_ref), custom_call_target="tpu_custom_call" | custom-call | tf_op jit(solution)/shard_map/pallas_call | solution.py:264
  49.6 0.0 copy-start.1
  49.6 1.3 %copy-done.1 = bf16[8,4,64,512]{3,2,1,0:T(8,128)(2,1)} copy-done((bf16[8,4,64,512]{3,2,1,0:T(8,128)(2,1)}, bf16[8,4,64,512]{3,2,1,0:T(8,128)(2,1)S(1)}, u32[]{:S(2)}) %copy-start.1) | copy-done | bytes 2097176
  51.0 9.8 %shard_map.103 = bf16[2048,512]{1,0:T(8,128)(2,1)} custom-call(s32[2048,1]{1,0:T(8,128)} %copy.13.g_ref, bf16[2048,2048]{1,0:T(8,128)(2,1)} %s_ref.1, bf16[2048,512]{1,0:T(8,128)(2,1)} %bitcast.7, bf16[512,512]{1,0:T(8,128)(2,1)} %a_ref.1), custom_call_target="tpu_custom_call" | custom-call | tf_op jit(solution)/shard_map/pallas_call | solution.py:292
  (1 shorter events, 0.0 us)
Async XLA Ops:
  0.0 1.6 %copy-start = (f32[256,2048]{1,0:T(8,128)S(1)}, f32[256,2048]{1,0:T(8,128)}, u32[]{:S(2)}) copy-start(f32[256,2048]{1,0:T(8,128)} %param.12) | copy-start | bytes 6291460
  0.0 13.1 %copy-start.2 = (bf16[256,256]{1,0:T(8,128)(2,1)S(1)}, bf16[256,256]{1,0:T(8,128)(2,1)}, u32[]{:S(2)}) copy-start(bf16[256,256]{1,0:T(8,128)(2,1)} %constant.21.clone.bl_ref) | copy-start | bytes 393220
  0.0 13.1 %copy-start.3 = (bf16[256,256]{1,0:T(8,128)(2,1)S(1)}, bf16[256,256]{1,0:T(8,128)(2,1)}, u32[]{:S(2)}) copy-start(bf16[256,256]{1,0:T(8,128)(2,1)} %constant.20.clone.bh_ref) | copy-start | bytes 393220
  0.0 13.2 %copy-start.4 = (bf16[128,256]{1,0:T(8,128)(2,1)S(1)}, bf16[128,256]{1,0:T(8,128)(2,1)}, u32[]{:S(2)}) copy-start(bf16[128,256]{1,0:T(8,128)(2,1)} %constant.19.clone.fl_ref) | copy-start | bytes 196612
  0.0 13.2 %copy-start.5 = (bf16[128,256]{1,0:T(8,128)(2,1)S(1)}, bf16[128,256]{1,0:T(8,128)(2,1)}, u32[]{:S(2)}) copy-start(bf16[128,256]{1,0:T(8,128)(2,1)} %constant.18.clone.fh_ref) | copy-start | bytes 196612
  1.6 14.2 %copy-start.6 = (s32[2048]{0:T(1024)S(1)}, s32[2048]{0:T(1024)}, u32[]{:S(2)}) copy-start(s32[2048]{0:T(1024)} %param.15) | copy-start | bytes 24580
  49.6 1.4 %copy-start.1 = (bf16[8,4,64,512]{3,2,1,0:T(8,128)(2,1)}, bf16[8,4,64,512]{3,2,1,0:T(8,128)(2,1)S(1)}, u32[]{:S(2)}) copy-start(bf16[8,4,64,512]{3,2,1,0:T(8,128)(2,1)S(1)} %shard_map.102) | copy-start | bytes 6291460
